TPU v7x, 32 devices: a whole 2x2x4 slice. The times are simulated.
32 devices in a mesh: axial: 8 (over y, x, core), azim: 4 (over z).
Axes of the slice: x: 2, y: 2, z: 4, core: 2. Of those that a mesh axis runs over, the one named last changes fastest.
Arguments:
- state: float32 [5, 16, 1024, 96], P(None, 'axial', 'azim'), as said below
- start: float32 [5, 16, 1024, 96], P(None, 'axial', 'azim'), as said below
- modes: int32 [64], replicated, may hold values from 1 to 512, as said below
Outputs:
- section: float32 [5, 16, 1024, 96], P(None, 'axial', 'azim')
Inputs may be any that keep to these rules, and one draw needn't show every extreme that they name: Cycle j keeps the modes 0 to modes[j] - 1; modes[j] lies between 8 * (j + 1) and 2 * 8 * (j + 1), capped at 512, which the last cycle reaches. `state`: the density (field 0) lies between 0.85 and 1.15. `start`: the density (field 0) lies between 0.85 and 1.15.
All inputs are finite; a program needn't handle non-finite values.
Results may differ from a plain program's by a relative error of at most 0.00005.
Values sent between devices are 32-bit elements; how exact they have to be, the bound alone decides.
A program may use at most 64 MiB of HBM per device.

v0:
```python
import math
import jax
import jax.numpy as jnp
from jax import lax
from jax.sharding import PartitionSpec as P

NTH = 1024
NIN = 64
GAMMA = 1.4
STEP_DT = 0.05


def swapped(value, axis, bit):
    return lax.ppermute(value, axis, [(i, i ^ 1 << bit) for i in range(lax.axis_size(axis))])


def with_halo(cells, sides, width):
    for axis, dim in sides:
        count = lax.axis_size(axis)
        head = lax.slice_in_dim(cells, 0, width, axis=dim)
        tail = lax.slice_in_dim(cells, cells.shape[dim] - width, cells.shape[dim], axis=dim)
        cells = jnp.concatenate(
            [
                lax.ppermute(tail, axis, [(i, (i + 1) % count) for i in range(count)]),
                cells,
                lax.ppermute(head, axis, [((i + 1) % count, i) for i in range(count)]),
            ],
            axis=dim,
        )
    return cells


def central_diff(values, dimension):
    length = values.shape[dimension] - 4

    def part_at(offset):
        return lax.slice_in_dim(values, offset, offset + length, axis=dimension)

    return (8.0 * (part_at(3) - part_at(1)) - (part_at(4) - part_at(0))) / 12.0


def pressure_of(values, inverse):
    kinetic = (values[1] * values[1] + values[2] * values[2] + values[3] * values[3]) * inverse
    return (GAMMA - 1.0) * (values[4] - 0.5 * kinetic)


def flux_along(values, direction):
    inverse = 1.0 / values[0]
    velocity = values[direction] * inverse
    pressure = pressure_of(values, inverse)
    components = [
        values[direction],
        values[1] * velocity,
        values[2] * velocity,
        values[3] * velocity,
        (values[4] + pressure) * velocity,
    ]
    components[direction] = components[direction] + pressure
    return jnp.stack(components)


def rates_of(padded, dtheta):
    axial_cells = padded[:, :, 2:-2, 2:-2]
    azimuth_cells = padded[:, 2:-2, :, 2:-2]
    radial_cells = padded[:, 2:-2, 2:-2, :]
    centre = padded[:, 2:-2, 2:-2, 2:-2]
    radius_all = jnp.arange(padded.shape[3], dtype=jnp.float32) - 1.5
    inv_radius = 1.0 / radius_all[2:-2]
    axial_term = central_diff(flux_along(axial_cells, 1), 1)
    radial_term = central_diff(flux_along(radial_cells, 2) * radius_all, 3) * inv_radius
    azimuth_term = central_diff(flux_along(azimuth_cells, 3), 2) * (inv_radius / dtheta)
    inverse = 1.0 / centre[0]
    pressure = pressure_of(centre, inverse)
    source_radial = (centre[3] * centre[3] * inverse + pressure) * inv_radius
    source_azimuth = -(centre[2] * centre[3] * inverse) * inv_radius
    totals = -(axial_term + radial_term + azimuth_term)
    return jnp.stack(
        [totals[0], totals[1], totals[2] + source_radial, totals[3] + source_azimuth, totals[4]]
    )


def radial_extend(haloed, partner):
    signs = jnp.array([1.0, 1.0, -1.0, -1.0, 1.0], dtype=jnp.float32).reshape(5, 1, 1, 1)
    ghost = jnp.flip(partner, 3) * signs
    rim_axial = (haloed.shape[1] - ghost.shape[1]) // 2
    rim_theta = (haloed.shape[2] - ghost.shape[2]) // 2
    ghost = jnp.pad(ghost, ((0, 0), (rim_axial, rim_axial), (rim_theta, rim_theta), (0, 0)))
    outer_cycles = jnp.repeat(haloed[..., -1:], 2, axis=3)
    return jnp.concatenate([ghost, haloed, outer_cycles], axis=3)


def fourier_tables():
    half_modes = NTH // 2
    mode_block = min(128, half_modes)
    block_count = half_modes // mode_block
    wavenumbers = jnp.arange(half_modes, dtype=jnp.int32)
    cell_numbers = jnp.arange(NTH, dtype=jnp.int32)
    phase_index = cell_numbers[:, None] * wavenumbers[None, :] % NTH
    angles = phase_index.astype(jnp.float32) * (2.0 * math.pi / NTH)
    cosines = jnp.cos(angles).reshape(NTH, block_count, mode_block).transpose(1, 0, 2)
    sines = jnp.sin(angles).reshape(NTH, block_count, mode_block).transpose(1, 0, 2)
    tables = jnp.concatenate([cosines, sines], axis=2)
    weights = (
        jnp.where(wavenumbers == 0, 1.0 / NTH, 2.0 / NTH)
        .astype(jnp.float32)
        .reshape(block_count, mode_block)
    )
    return (tables, weights, wavenumbers.reshape(block_count, mode_block), mode_block)


def truncate_cycles(slab, local_modes, tables, weights, wave_blocks, mode_block):

    def one_cycle(cycle_index, result):
        cycle_values = lax.dynamic_index_in_dim(slab, cycle_index, 1, keepdims=False)
        mode_count = lax.dynamic_index_in_dim(local_modes, cycle_index, 0, keepdims=False)
        used_blocks = (mode_count + mode_block - 1) // mode_block

        def one_block(block_index, series_sum):
            basis_block = lax.dynamic_index_in_dim(tables, block_index, 0, keepdims=False)
            coeffs = jnp.dot(cycle_values, basis_block, precision=lax.Precision.HIGHEST)
            block_waves = lax.dynamic_index_in_dim(wave_blocks, block_index, 0, keepdims=False)
            block_weights = lax.dynamic_index_in_dim(weights, block_index, 0, keepdims=False)
            kept_weights = jnp.where(block_waves < mode_count, block_weights, 0.0)
            scaled = coeffs * jnp.concatenate([kept_weights, kept_weights])
            return series_sum + lax.dot_general(
                scaled, basis_block, (((1,), (1,)), ((), ())), precision=lax.Precision.HIGHEST
            )

        series = lax.fori_loop(
            0, used_blocks, one_block, jnp.zeros(cycle_values.shape, jnp.float32)
        )
        return lax.dynamic_update_index_in_dim(result, series, cycle_index, 1)

    return lax.fori_loop(0, slab.shape[1], one_cycle, jnp.zeros(slab.shape, jnp.float32))


def shards(state, start, modes):
    field_count, axial_local, theta_local, cycle_total = state.shape
    azim_size = lax.axis_size("azim")
    azim_index = lax.axis_index("azim")
    cycles_local = NIN // azim_size
    item_count = field_count * axial_local
    tables, weights, wave_blocks, mode_block = fourier_tables()
    inner = state[..., :NIN].transpose(0, 1, 3, 2).reshape(item_count, NIN, theta_local)
    local_modes = lax.dynamic_slice_in_dim(modes, azim_index * cycles_local, cycles_local)
    smoothed = truncate_cycles(
        lax.all_to_all(inner, "azim", split_axis=1, concat_axis=2, tiled=True),
        local_modes,
        tables,
        weights,
        wave_blocks,
        mode_block,
    )
    exchanged = lax.all_to_all(smoothed, "azim", split_axis=2, concat_axis=1, tiled=True)
    smooth_inner = exchanged.reshape(field_count, axial_local, NIN, theta_local).transpose(
        0, 1, 3, 2
    )
    smoothed_state = jnp.concatenate([smooth_inner, state[..., NIN:]], axis=3)
    partner = swapped(smoothed_state[..., :2], "azim", azim_size.bit_length() - 2)
    haloed = with_halo(smoothed_state, (("axial", 1), ("azim", 2)), 2)
    padded = radial_extend(haloed, partner)
    rate = rates_of(padded, 2.0 * math.pi / NTH)
    return start + STEP_DT * rate


def solution(mesh):
    in_specs = (P(None, "axial", "azim", None), P(None, "axial", "azim", None), P())
    out_specs = P(None, "axial", "azim", None)
    return jax.shard_map(shards, mesh=mesh, in_specs=in_specs, out_specs=out_specs, check_vma=False)
```

profile of v0, /device:TPU:0, one launch (start us, length us, event | category | flops | bytes accessed | tf_op | source)
XLA Modules:
  0.0 475.3 jit_solution(14893907723052022930)
XLA Ops:
  2.6 6.3 %all-to-all-start = ((f32[10,64,256]{2,0,1:T(8,128)}), f32[10,64,256]{2,0,1:T(8,128)S(1)}, u32[]{:S(2)}, u32[]{:S(2)}) async-start(f32[10,64,256]{2,0,1:T(8,128)} %copy.27), calls=%async_computation | async-start | bytes 2097152 | tf_op jit(solution)/shard_map/all_to_all | solution.py:147
  9.0 8.1 %fusion.19 = (f32[4,1024,128]{2,1,0:T(8,128)S(1)}, f32[4,1024,128]{2,1,0:T(8,128)S(1)}) fusion(s32[4,128]{1,0:T(4,128)S(1)} %multiply_add_fusion.1), kind=kLoop, calls=%fused_computation.45 | loop fusion | flops 7340032 | bytes 4196352 | tf_op jit(solution)/shard_map/cos | solution.py:100
  17.1 2.2 pad_maximum_fusion.1
  19.4 15.3 %all-to-all-done = f32[10,64,256]{2,0,1:T(8,128)S(1)} async-done(((f32[10,64,256]{2,0,1:T(8,128)}), f32[10,64,256]{2,0,1:T(8,128)S(1)}, u32[]{:S(2)}, u32[]{:S(2)}) %all-to-all-start) | async-done | bytes 655392 | tf_op jit(solution)/shard_map/all_to_all | solution.py:147
  35.4 122.0 %while.64 = (s32[]{:T(128)}, f32[10,16,1024]{2,0,1:T(8,128)}, s32[16]{0:T(128)S(1)}, f32[10,16,1024]{2,0,1:T(8,128)S(1)}, f32[4,1024,256]{2,1,0:T(8,128)}, /*ind...) while((s32[]{:T(128)}, f32[10,16,1024]{2,0,1:T(8,128)}, ...), condition=%wide.region_3.4_spmd.clone, body=%wide.region_0.3_spmd.clone.sunk | while | flops 62930964 | bytes 2478670 | solution.py:134
  36.6 4.6 while.65
  37.2 1.8 convolution_multiply_fusion.2
  39.1 2.2 convolution_add_fusion.2
  43.1 4.6 while.65
  43.7 1.8 convolution_multiply_fusion.2
  45.5 2.2 convolution_add_fusion.2
  49.6 4.6 while.65
  50.2 1.8 convolution_multiply_fusion.2
  52.0 2.2 convolution_add_fusion.2
  56.0 4.6 while.65
  56.6 1.8 convolution_multiply_fusion.2
  58.5 2.2 convolution_add_fusion.2
  62.5 4.6 while.65
  63.1 1.8 convolution_multiply_fusion.2
  64.9 2.2 convolution_add_fusion.2
  69.0 4.6 while.65
  69.6 1.8 convolution_multiply_fusion.2
  71.4 2.2 convolution_add_fusion.2
  75.4 4.6 while.65
  76.0 1.8 convolution_multiply_fusion.2
  77.9 2.2 convolution_add_fusion.2
  81.9 4.6 while.65
  82.5 1.8 convolution_multiply_fusion.2
  84.3 2.2 convolution_add_fusion.2
  88.4 4.6 while.65
  89.0 1.8 convolution_multiply_fusion.2
  90.8 2.2 convolution_add_fusion.2
  94.8 4.6 while.65
  95.4 1.8 convolution_multiply_fusion.2
  97.3 2.2 convolution_add_fusion.2
  101.3 4.6 while.65
  103.7 2.2 convolution_add_fusion.2
  107.8 9.3 %while.65 = (s32[]{:T(128)}, f32[10,1024]{1,0:T(8,128)S(1)}, s32[]{:T(128)}, f32[4,1024,256]{2,1,0:T(8,128)}, f32[10,1024]{1,0:T(8,128)S(1)}, /*index=5*/s32[4,1...) while((s32[]{:T(128)}, f32[10,1024]{1,0:T(8,128)S(1)}, ...), condition=%wide.region_2.2_spmd, body=%wide.region_1.1_spmd.sunk | while | flops 62927876 | bytes 2244775 | solution.py:129
  110.2 2.2 convolution_add_fusion.2
  114.8 2.2 convolution_add_fusion.2
  118.9 9.3 %while.65 = (s32[]{:T(128)}, f32[10,1024]{1,0:T(8,128)S(1)}, s32[]{:T(128)}, f32[4,1024,256]{2,1,0:T(8,128)}, f32[10,1024]{1,0:T(8,128)S(1)}, /*index=5*/s32[4,1...) while((s32[]{:T(128)}, f32[10,1024]{1,0:T(8,128)S(1)}, ...), condition=%wide.region_2.2_spmd, body=%wide.region_1.1_spmd.sunk | while | flops 62927876 | bytes 2244775 | solution.py:129
  121.3 2.2 convolution_add_fusion.2
  125.9 2.2 convolution_add_fusion.2
  130.0 4.6 while.65
  132.4 2.2 convolution_add_fusion.2
  136.4 9.3 %while.65 = (s32[]{:T(128)}, f32[10,1024]{1,0:T(8,128)S(1)}, s32[]{:T(128)}, f32[4,1024,256]{2,1,0:T(8,128)}, f32[10,1024]{1,0:T(8,128)S(1)}, /*index=5*/s32[4,1...) while((s32[]{:T(128)}, f32[10,1024]{1,0:T(8,128)S(1)}, ...), condition=%wide.region_2.2_spmd, body=%wide.region_1.1_spmd.sunk | while | flops 62927876 | bytes 2244775 | solution.py:129
  138.9 2.2 convolution_add_fusion.2
  143.5 2.2 convolution_add_fusion.2
  147.5 9.3 %while.65 = (s32[]{:T(128)}, f32[10,1024]{1,0:T(8,128)S(1)}, s32[]{:T(128)}, f32[4,1024,256]{2,1,0:T(8,128)}, f32[10,1024]{1,0:T(8,128)S(1)}, /*index=5*/s32[4,1...) while((s32[]{:T(128)}, f32[10,1024]{1,0:T(8,128)S(1)}, ...), condition=%wide.region_2.2_spmd, body=%wide.region_1.1_spmd.sunk | while | flops 62927876 | bytes 2244775 | solution.py:129
  150.0 2.2 convolution_add_fusion.2
  154.6 2.2 convolution_add_fusion.2
  157.5 7.1 %copy.31 = f32[10,16,1024]{0,1,2:T(8,128)} copy(f32[10,16,1024]{2,0,1:T(8,128)} %get-tuple-element.299) | data formatting | bytes 1310720 | tf_op jit(solution)/shard_map/while | solution.py:134
  164.6 9.5 %reshape.52 = f32[4,1,40960]{2,1,0:T(1,128)} reshape(f32[1024,16,10]{2,1,0:T(8,128)} %bitcast.58) | data formatting | bytes 1310720
  174.0 206.8 %all-to-all-start.1 = ((f32[4,1,40960]{2,1,0:T(1,128)}), f32[4,1,40960]{2,1,0:T(1,128)S(1)}, u32[]{:S(2)}, u32[]{:S(2)}) async-start(f32[4,1,40960]{2,1,0:T(1,128)} %reshape.52), calls=%async_computation.1 | async-start | bytes 1310720 | tf_op jit(solution)/shard_map/all_to_all | solution.py:154
  381.9 15.2 %all-to-all-done.1 = f32[4,1,40960]{2,1,0:T(1,128)S(1)} async-done(((f32[4,1,40960]{2,1,0:T(1,128)}), f32[4,1,40960]{2,1,0:T(1,128)S(1)}, u32[]{:S(2)}, u32[]{:S(2)}) %all-to-all-start.1) | async-done | bytes 655392 | tf_op jit(solution)/shard_map/all_to_all | solution.py:154
  397.6 2.5 reduce
  400.1 12.5 %reshape.53 = f32[1024,16,10]{2,1,0:T(8,128)} reshape(f32[4,40960]{1,0:T(4,128)S(1)} %reduce) | data formatting | bytes 1310720
  412.6 5.4 %copy.40 = f32[10,16,4,256]{3,2,1,0:T(4,128)S(1)} copy(f32[10,16,4,256]{0,1,3,2:T(8,128)} %bitcast.59) | data formatting | bytes 1310720 | tf_op jit(solution)/shard_map/all_to_all | solution.py:154
  420.6 4.7 collective-permute-done.2
  425.5 17.2 %collective-permute-done.1 = f32[5,2,256,96]{2,3,1,0:T(8,128)S(1)} collective-permute-done((f32[5,2,256,96]{2,3,1,0:T(8,128)}, f32[5,2,256,96]{2,3,1,0:T(8,128)S(1)}, u32[]{:S(2)}, u32[]{:S(2)}) %collective-permute-start.1) | collective-permute-done | bytes 983072 | tf_op jit(solution)/shard_map/ppermute | solution.py:26
  442.7 1.9 collective-permute-done
  445.5 2.5 fusion.49
  448.9 2.0 copy.35
  462.4 6.0 %fusion.11 = f32[5,6,260,100]{2,3,1,0:T(8,128)S(1)} fusion(f32[5,2,256,2]{2,3,1,0:T(2,128)S(1)} %broadcast_multiply_fusion.1, f32[5,6,260,2]{2,3,1,0:T(2,128)S(1)} %reshape.50, f32[5,6,2,96]{2,3,1,0:T(8,128)S(1)} %copy.37, f32[5,2,256,96]{2,3,1,0:T(8,128)S(1)} %copy-done.3, f32[5,2,256,32]{2,3,1,0:T(8,128)S(1)} %slice.186, ...), kind=kLoop, calls=%fused_computation.20 | loop fusion | flops 7020000 | bytes 6198080 | tf_op jit(solution)/shard_map/concatenate | solution.py:89
  (221 shorter events, 76.7 us)
Async XLA Ops:
  1.1 7.8 %copy-start.11 = (s32[64]{0:T(128)S(1)}, s32[64]{0:T(128)}, u32[]{:S(2)}) copy-start(s32[64]{0:T(128)} %param.10) | copy-start | bytes 772
  2.6 32.1 %all-to-all-start = ((f32[10,64,256]{2,0,1:T(8,128)}), f32[10,64,256]{2,0,1:T(8,128)S(1)}, u32[]{:S(2)}, u32[]{:S(2)}) async-start(f32[10,64,256]{2,0,1:T(8,128)} %copy.27), calls=%async_computation | async-start | bytes 2097152 | tf_op jit(solution)/shard_map/all_to_all | solution.py:147
  174.0 223.0 %all-to-all-start.1 = ((f32[4,1,40960]{2,1,0:T(1,128)}), f32[4,1,40960]{2,1,0:T(1,128)S(1)}, u32[]{:S(2)}, u32[]{:S(2)}) async-start(f32[4,1,40960]{2,1,0:T(1,128)} %reshape.52), calls=%async_computation.1 | async-start | bytes 1310720 | tf_op jit(solution)/shard_map/all_to_all | solution.py:154
  418.0 7.4 %copy-start.10 = (f32[5]{0:T(128)S(1)}, f32[5]{0:T(128)}, u32[]{:S(2)}) copy-start(f32[5]{0:T(128)} %constant.217.clone) | copy-start | bytes 64
  418.1 26.6 %copy-start = (f32[10,4,16,256]{3,2,1,0:T(8,128)}, f32[10,4,16,256]{3,2,1,0:T(8,128)S(1)}, u32[]{:S(2)}) copy-start(f32[10,4,16,256]{3,2,1,0:T(8,128)S(1)} %copy.33) | copy-start | bytes 1966084
  419.3 23.4 %collective-permute-start.1 = (f32[5,2,256,96]{2,3,1,0:T(8,128)}, f32[5,2,256,96]{2,3,1,0:T(8,128)S(1)}, u32[]{:S(2)}, u32[]{:S(2)}) collective-permute-start(f32[5,2,256,96]{2,3,1,0:T(8,128)} %pad_maximum_fusion.3), channel_id=1, source_target_pairs={{4,0},{8,4},{12,8},{16,12},{20,16},{24,20},{28,24},{0,28},{5,1},{9... | collective-permute-start | bytes 2949128 | tf_op jit(solution)/shard_map/ppermute | solution.py:26
  420.4 24.1 %collective-permute-start = (f32[5,2,256,96]{2,3,1,0:T(8,128)}, f32[5,2,256,96]{2,3,1,0:T(8,128)S(1)}, u32[]{:S(2)}, u32[]{:S(2)}) collective-permute-start(f32[5,2,256,96]{2,3,1,0:T(8,128)} %pad_maximum_fusion.3), channel_id=1, source_target_pairs={{0,4},{4,8},{8,12},{12,16},{16,20},{20,24},{24,28},{28,0},{1,5},{5... | collective-permute-start | bytes 2949128 | tf_op jit(solution)/shard_map/ppermute | solution.py:24
  420.5 4.7 collective-permute-start.2
  442.7 2.1 copy-start.2
  444.5 0.9 copy-start.4
  445.5 2.5 copy-start.6
  448.9 6.1 %copy-start.7 = (f32[5,6,256,96]{2,3,1,0:T(8,128)S(1)}, f32[5,6,256,96]{2,3,1,0:T(8,128)}, u32[]{:S(2)}) copy-start(f32[5,6,256,96]{2,3,1,0:T(8,128)} %copy-done.6) | copy-start | bytes 8847364
  450.8 8.0 %collective-permute-start.4 = (f32[5,6,2,96]{3,2,1,0:T(2,128)S(1)}, f32[5,6,2,96]{3,2,1,0:T(2,128)S(1)}, u32[]{:S(2)}, u32[]{:S(2)}) collective-permute-start(f32[5,6,2,96]{3,2,1,0:T(2,128)S(1)} %copy.35), channel_id=1, source_target_pairs={{1,0},{2,1},{3,2},{0,3},{5,4},{6,5},{7,6},{4,7},{9,8},{10,9},{11,1... | collective-permute-start | bytes 69128 | tf_op jit(solution)/shard_map/ppermute | solution.py:26
  454.2 5.9 %collective-permute-start.3 = (f32[5,6,2,96]{3,2,1,0:T(2,128)S(1)}, f32[5,6,2,96]{3,2,1,0:T(2,128)S(1)}, u32[]{:S(2)}, u32[]{:S(2)}) collective-permute-start(f32[5,6,2,96]{3,2,1,0:T(2,128)S(1)} %copy.34), channel_id=1, source_target_pairs={{0,1},{1,2},{2,3},{3,0},{4,5},{5,6},{6,7},{7,4},{8,9},{9,10},{10,1... | collective-permute-start | bytes 69128 | tf_op jit(solution)/shard_map/ppermute | solution.py:24
  460.6 1.4 copy-start.1
  460.6 1.5 copy-start.3
  460.6 1.8 copy-start.5
  470.2 1.8 copy-start.8
  473.0 1.2 copy-start.9
where the time goes:
time: 481 us; the launch traced here: 475 us
  starting transfers between devices  217 us (45%)
  matrix products  80.6 us (17%)
  local copies, waits for them, and re-layouts  70.8 us (15%)
  waiting for transfers between devices  54.9 us (11%)
  other arithmetic  41 us (9%)
  loops' own time  10.8 us (2%)
    all_to_all x1, starting transfers between devices, shards(): lax.all_to_all(smoothed, 'azim', split_axis=2, concat_axis=1, tiled=True)  207 us
    dot_general x20, matrix products, one_block(): lax.dot_general(scaled, basis_block, (((1,), (1,)), ((), ())), precision=...  43.9 us
    dot_general x20, matrix products, one_block(): coeffs = jnp.dot(cycle_values, basis_block, precision=lax.Precision.HIGHEST)  36.7 us
    unnamed x31, local copies, waits for them, and re-layouts  27.4 us
    ppermute x2, waiting for transfers between devices, with_halo(): lax.ppermute(head, axis, [((i + 1) % count, i) for i in range(count)])  17.2 us
    all_to_all x1, waiting for transfers between devices, shards(): lax.all_to_all(inner, 'azim', split_axis=1, concat_axis=2, tiled=True)  15.3 us
    all_to_all x1, waiting for transfers between devices, shards(): lax.all_to_all(smoothed, 'azim', split_axis=2, concat_axis=1, tiled=True)  15.2 us
    select_n x20, other arithmetic, one_block(): kept_weights = jnp.where(block_waves < mode_count, block_weights, 0.0)  11.1 us
  transfers between devices with their start and end apart: 7, of which 6 were waited for; matrix products, arithmetic and copies ran while one was open for 4% of the time, Pallas kernels for 0%

commit v1 on v0

--- a/solution.py
+++ b/solution.py
@@ -151,7 +151,10 @@
         wave_blocks,
         mode_block,
     )
-    exchanged = lax.all_to_all(smoothed, "azim", split_axis=2, concat_axis=1, tiled=True)
+    exchanged = jnp.concatenate(
+        lax.all_to_all(jnp.stack(jnp.split(smoothed, lax.axis_size("azim"), axis=2)), "azim", 0, 0),
+        axis=1,
+    )
     smooth_inner = exchanged.reshape(field_count, axial_local, NIN, theta_local).transpose(
         0, 1, 3, 2
     )

time: 481 us -> 445 us (0.925)
  local copies, waits for them, and re-layouts: 70.8 us -> 34.8 us
    unnamed x31 -> x29, local copies, waits for them, and re-layouts: 27.4 us -> 5.49 us
    while x1 -> x0, local copies, waits for them, and re-layouts: 7.12 us -> none  [truncate_cycles(): lax.fori_loop(0, slab.shape[1], one_cycle, jnp.zeros(slab.shape, jnp.floa...]
    all_to_all x3 -> x1, local copies, waits for them, and re-layouts: 6.03 us -> 0.05 us  [shards(): lax.all_to_all(jnp.stack(jnp.split(smoothed, lax.axis_size('azim'), axis=...]
    dynamic_update_slice x16 -> x32, local copies, waits for them, and re-layouts: 10 us -> 8.49 us  [one_cycle(): return lax.dynamic_update_index_in_dim(result, series, cycle_index, 1)]
where the time goes in v1:
time: 445 us; the launch traced here: 439 us
  starting transfers between devices  217 us (49%)
  matrix products  80.6 us (18%)
  waiting for transfers between devices  54.9 us (12%)
  other arithmetic  39.7 us (9%)
  local copies, waits for them, and re-layouts  34.8 us (8%)
  loops' own time  11.5 us (3%)
    all_to_all x1, starting transfers between devices, shards(): lax.all_to_all(jnp.stack(jnp.split(smoothed, lax.axis_size('azim'), axis=...  208 us
    dot_general x20, matrix products, one_block(): lax.dot_general(scaled, basis_block, (((1,), (1,)), ((), ())), precision=...  43.9 us
    dot_general x20, matrix products, one_block(): coeffs = jnp.dot(cycle_values, basis_block, precision=lax.Precision.HIGHEST)  36.7 us
    ppermute x2, waiting for transfers between devices, with_halo(): lax.ppermute(head, axis, [((i + 1) % count, i) for i in range(count)])  17.2 us
    all_to_all x1, waiting for transfers between devices, shards(): lax.all_to_all(inner, 'azim', split_axis=1, concat_axis=2, tiled=True)  15.3 us
    all_to_all x1, waiting for transfers between devices, shards(): lax.all_to_all(jnp.stack(jnp.split(smoothed, lax.axis_size('azim'), axis=...  15.1 us
    select_n x20, other arithmetic, one_block(): kept_weights = jnp.where(block_waves < mode_count, block_weights, 0.0)  11.4 us
    another operation x1, loops' own time, truncate_cycles(): lax.fori_loop(0, slab.shape[1], one_cycle, jnp.zeros(slab.shape, jnp.floa...  10.5 us
  transfers between devices with their start and end apart: 7, of which 6 were waited for; matrix products, arithmetic and copies ran while one was open for 4% of the time, Pallas kernels for 0%

profile of v1, /device:TPU:0, one launch (start us, length us, event | category | flops | bytes accessed | tf_op | source)
XLA Modules:
  0.0 439.0 jit_solution(7469195461948029456)
XLA Ops:
  2.6 6.3 %all-to-all-start = ((f32[10,64,256]{2,0,1:T(8,128)}), f32[10,64,256]{2,0,1:T(8,128)S(1)}, u32[]{:S(2)}, u32[]{:S(2)}) async-start(f32[10,64,256]{2,0,1:T(8,128)} %copy.30), calls=%async_computation | async-start | bytes 2097152 | tf_op jit(solution)/shard_map/all_to_all | solution.py:147
  9.0 8.1 %fusion.19 = (f32[4,1024,128]{2,1,0:T(8,128)S(1)}, f32[4,1024,128]{2,1,0:T(8,128)S(1)}) fusion(s32[4,128]{1,0:T(4,128)S(1)} %multiply_add_fusion.1), kind=kLoop, calls=%fused_computation.44 | loop fusion | flops 7340032 | bytes 4196352 | tf_op jit(solution)/shard_map/cos | solution.py:100
  17.1 2.2 pad_maximum_fusion.1
  19.4 15.3 %all-to-all-done = f32[10,64,256]{2,0,1:T(8,128)S(1)} async-done(((f32[10,64,256]{2,0,1:T(8,128)}), f32[10,64,256]{2,0,1:T(8,128)S(1)}, u32[]{:S(2)}, u32[]{:S(2)}) %all-to-all-start) | async-done | bytes 655392 | tf_op jit(solution)/shard_map/all_to_all | solution.py:147
  35.5 122.0 %while.64 = (s32[]{:T(128)}, f32[10,16,1024]{2,1,0:T(8,128)S(1)}, s32[16]{0:T(128)S(1)}, f32[10,16,1024]{2,0,1:T(8,128)S(1)}, f32[4,1024,256]{2,1,0:T(8,128)}, /...) while((s32[]{:T(128)}, f32[10,16,1024]{2,1,0:T(8,128)S(1)}, ...), condition=%wide.region_3.4_spmd.clone, body=%wide.region_0.3_spmd.clone.sunk | while | flops 62930964 | bytes 2536014 | solution.py:134
  36.7 4.7 %while.65 = (s32[]{:T(128)}, f32[10,1024]{1,0:T(8,128)S(1)}, s32[]{:T(128)}, f32[4,1024,256]{2,1,0:T(8,128)}, f32[10,1024]{1,0:T(8,128)S(1)}, /*index=5*/s32[4,1...) while((s32[]{:T(128)}, f32[10,1024]{1,0:T(8,128)S(1)}, ...), condition=%wide.region_2.2_spmd, body=%wide.region_1.1_spmd.sunk | while | flops 62927876 | bytes 2244775 | solution.py:129
  37.3 1.8 convolution_multiply_fusion.2
  39.2 2.2 convolution_add_fusion.2
  43.2 4.7 %while.65 = (s32[]{:T(128)}, f32[10,1024]{1,0:T(8,128)S(1)}, s32[]{:T(128)}, f32[4,1024,256]{2,1,0:T(8,128)}, f32[10,1024]{1,0:T(8,128)S(1)}, /*index=5*/s32[4,1...) while((s32[]{:T(128)}, f32[10,1024]{1,0:T(8,128)S(1)}, ...), condition=%wide.region_2.2_spmd, body=%wide.region_1.1_spmd.sunk | while | flops 62927876 | bytes 2244775 | solution.py:129
  43.8 1.8 convolution_multiply_fusion.2
  45.6 2.2 convolution_add_fusion.2
  49.6 4.7 %while.65 = (s32[]{:T(128)}, f32[10,1024]{1,0:T(8,128)S(1)}, s32[]{:T(128)}, f32[4,1024,256]{2,1,0:T(8,128)}, f32[10,1024]{1,0:T(8,128)S(1)}, /*index=5*/s32[4,1...) while((s32[]{:T(128)}, f32[10,1024]{1,0:T(8,128)S(1)}, ...), condition=%wide.region_2.2_spmd, body=%wide.region_1.1_spmd.sunk | while | flops 62927876 | bytes 2244775 | solution.py:129
  50.2 1.8 convolution_multiply_fusion.2
  52.1 2.2 convolution_add_fusion.2
  56.1 4.7 %while.65 = (s32[]{:T(128)}, f32[10,1024]{1,0:T(8,128)S(1)}, s32[]{:T(128)}, f32[4,1024,256]{2,1,0:T(8,128)}, f32[10,1024]{1,0:T(8,128)S(1)}, /*index=5*/s32[4,1...) while((s32[]{:T(128)}, f32[10,1024]{1,0:T(8,128)S(1)}, ...), condition=%wide.region_2.2_spmd, body=%wide.region_1.1_spmd.sunk | while | flops 62927876 | bytes 2244775 | solution.py:129
  56.7 1.8 convolution_multiply_fusion.2
  58.5 2.2 convolution_add_fusion.2
  62.5 4.7 %while.65 = (s32[]{:T(128)}, f32[10,1024]{1,0:T(8,128)S(1)}, s32[]{:T(128)}, f32[4,1024,256]{2,1,0:T(8,128)}, f32[10,1024]{1,0:T(8,128)S(1)}, /*index=5*/s32[4,1...) while((s32[]{:T(128)}, f32[10,1024]{1,0:T(8,128)S(1)}, ...), condition=%wide.region_2.2_spmd, body=%wide.region_1.1_spmd.sunk | while | flops 62927876 | bytes 2244775 | solution.py:129
  63.1 1.8 convolution_multiply_fusion.2
  65.0 2.2 convolution_add_fusion.2
  69.0 4.7 %while.65 = (s32[]{:T(128)}, f32[10,1024]{1,0:T(8,128)S(1)}, s32[]{:T(128)}, f32[4,1024,256]{2,1,0:T(8,128)}, f32[10,1024]{1,0:T(8,128)S(1)}, /*index=5*/s32[4,1...) while((s32[]{:T(128)}, f32[10,1024]{1,0:T(8,128)S(1)}, ...), condition=%wide.region_2.2_spmd, body=%wide.region_1.1_spmd.sunk | while | flops 62927876 | bytes 2244775 | solution.py:129
  69.6 1.8 convolution_multiply_fusion.2
  71.5 2.2 convolution_add_fusion.2
  75.5 4.7 %while.65 = (s32[]{:T(128)}, f32[10,1024]{1,0:T(8,128)S(1)}, s32[]{:T(128)}, f32[4,1024,256]{2,1,0:T(8,128)}, f32[10,1024]{1,0:T(8,128)S(1)}, /*index=5*/s32[4,1...) while((s32[]{:T(128)}, f32[10,1024]{1,0:T(8,128)S(1)}, ...), condition=%wide.region_2.2_spmd, body=%wide.region_1.1_spmd.sunk | while | flops 62927876 | bytes 2244775 | solution.py:129
  76.1 1.8 convolution_multiply_fusion.2
  77.9 2.2 convolution_add_fusion.2
  81.9 4.7 %while.65 = (s32[]{:T(128)}, f32[10,1024]{1,0:T(8,128)S(1)}, s32[]{:T(128)}, f32[4,1024,256]{2,1,0:T(8,128)}, f32[10,1024]{1,0:T(8,128)S(1)}, /*index=5*/s32[4,1...) while((s32[]{:T(128)}, f32[10,1024]{1,0:T(8,128)S(1)}, ...), condition=%wide.region_2.2_spmd, body=%wide.region_1.1_spmd.sunk | while | flops 62927876 | bytes 2244775 | solution.py:129
  82.5 1.8 convolution_multiply_fusion.2
  84.4 2.2 convolution_add_fusion.2
  88.4 4.7 %while.65 = (s32[]{:T(128)}, f32[10,1024]{1,0:T(8,128)S(1)}, s32[]{:T(128)}, f32[4,1024,256]{2,1,0:T(8,128)}, f32[10,1024]{1,0:T(8,128)S(1)}, /*index=5*/s32[4,1...) while((s32[]{:T(128)}, f32[10,1024]{1,0:T(8,128)S(1)}, ...), condition=%wide.region_2.2_spmd, body=%wide.region_1.1_spmd.sunk | while | flops 62927876 | bytes 2244775 | solution.py:129
  89.0 1.8 convolution_multiply_fusion.2
  90.8 2.2 convolution_add_fusion.2
  94.8 4.7 %while.65 = (s32[]{:T(128)}, f32[10,1024]{1,0:T(8,128)S(1)}, s32[]{:T(128)}, f32[4,1024,256]{2,1,0:T(8,128)}, f32[10,1024]{1,0:T(8,128)S(1)}, /*index=5*/s32[4,1...) while((s32[]{:T(128)}, f32[10,1024]{1,0:T(8,128)S(1)}, ...), condition=%wide.region_2.2_spmd, body=%wide.region_1.1_spmd.sunk | while | flops 62927876 | bytes 2244775 | solution.py:129
  95.4 1.8 convolution_multiply_fusion.2
  97.3 2.2 convolution_add_fusion.2
  101.3 4.7 %while.65 = (s32[]{:T(128)}, f32[10,1024]{1,0:T(8,128)S(1)}, s32[]{:T(128)}, f32[4,1024,256]{2,1,0:T(8,128)}, f32[10,1024]{1,0:T(8,128)S(1)}, /*index=5*/s32[4,1...) while((s32[]{:T(128)}, f32[10,1024]{1,0:T(8,128)S(1)}, ...), condition=%wide.region_2.2_spmd, body=%wide.region_1.1_spmd.sunk | while | flops 62927876 | bytes 2244775 | solution.py:129
  101.9 1.8 convolution_multiply_fusion.2
  103.7 2.2 convolution_add_fusion.2
  107.7 9.3 %while.65 = (s32[]{:T(128)}, f32[10,1024]{1,0:T(8,128)S(1)}, s32[]{:T(128)}, f32[4,1024,256]{2,1,0:T(8,128)}, f32[10,1024]{1,0:T(8,128)S(1)}, /*index=5*/s32[4,1...) while((s32[]{:T(128)}, f32[10,1024]{1,0:T(8,128)S(1)}, ...), condition=%wide.region_2.2_spmd, body=%wide.region_1.1_spmd.sunk | while | flops 62927876 | bytes 2244775 | solution.py:129
  108.4 1.8 convolution_multiply_fusion.2
  110.2 2.2 convolution_add_fusion.2
  113.0 1.8 convolution_multiply_fusion.2
  114.9 2.2 convolution_add_fusion.2
  118.9 9.3 %while.65 = (s32[]{:T(128)}, f32[10,1024]{1,0:T(8,128)S(1)}, s32[]{:T(128)}, f32[4,1024,256]{2,1,0:T(8,128)}, f32[10,1024]{1,0:T(8,128)S(1)}, /*index=5*/s32[4,1...) while((s32[]{:T(128)}, f32[10,1024]{1,0:T(8,128)S(1)}, ...), condition=%wide.region_2.2_spmd, body=%wide.region_1.1_spmd.sunk | while | flops 62927876 | bytes 2244775 | solution.py:129
  121.3 2.2 convolution_add_fusion.2
  126.0 2.2 convolution_add_fusion.2
  130.0 4.7 %while.65 = (s32[]{:T(128)}, f32[10,1024]{1,0:T(8,128)S(1)}, s32[]{:T(128)}, f32[4,1024,256]{2,1,0:T(8,128)}, f32[10,1024]{1,0:T(8,128)S(1)}, /*index=5*/s32[4,1...) while((s32[]{:T(128)}, f32[10,1024]{1,0:T(8,128)S(1)}, ...), condition=%wide.region_2.2_spmd, body=%wide.region_1.1_spmd.sunk | while | flops 62927876 | bytes 2244775 | solution.py:129
  130.6 1.8 convolution_multiply_fusion.2
  132.4 2.2 convolution_add_fusion.2
  136.4 9.3 %while.65 = (s32[]{:T(128)}, f32[10,1024]{1,0:T(8,128)S(1)}, s32[]{:T(128)}, f32[4,1024,256]{2,1,0:T(8,128)}, f32[10,1024]{1,0:T(8,128)S(1)}, /*index=5*/s32[4,1...) while((s32[]{:T(128)}, f32[10,1024]{1,0:T(8,128)S(1)}, ...), condition=%wide.region_2.2_spmd, body=%wide.region_1.1_spmd.sunk | while | flops 62927876 | bytes 2244775 | solution.py:129
  138.9 2.2 convolution_add_fusion.2
  141.7 1.8 convolution_multiply_fusion.2
  143.5 2.2 convolution_add_fusion.2
  147.5 9.3 %while.65 = (s32[]{:T(128)}, f32[10,1024]{1,0:T(8,128)S(1)}, s32[]{:T(128)}, f32[4,1024,256]{2,1,0:T(8,128)}, f32[10,1024]{1,0:T(8,128)S(1)}, /*index=5*/s32[4,1...) while((s32[]{:T(128)}, f32[10,1024]{1,0:T(8,128)S(1)}, ...), condition=%wide.region_2.2_spmd, body=%wide.region_1.1_spmd.sunk | while | flops 62927876 | bytes 2244775 | solution.py:129
  150.0 2.2 convolution_add_fusion.2
  154.7 2.2 convolution_add_fusion.2
  158.4 207.5 %all-to-all-start.1 = ((f32[4,10,16,256]{3,2,1,0:T(8,128)}), f32[4,10,16,256]{3,2,1,0:T(8,128)S(1)}, u32[]{:S(2)}, u32[]{:S(2)}) async-start(f32[4,10,16,256]{3,2,1,0:T(8,128)} %pad_maximum_fusion.4), calls=%async_computation.1 | async-start | bytes 1310720 | tf_op jit(solution)/shard_map/all_to_all | solution.py:155
  366.9 15.1 %all-to-all-done.1 = f32[4,10,16,256]{3,2,1,0:T(8,128)S(1)} async-done(((f32[4,10,16,256]{3,2,1,0:T(8,128)}), f32[4,10,16,256]{3,2,1,0:T(8,128)S(1)}, u32[]{:S(2)}, u32[]{:S(2)}) %all-to-all-start.1) | async-done | bytes 655392 | tf_op jit(solution)/shard_map/all_to_all | solution.py:155
  384.6 4.7 %collective-permute-done.2 = f32[5,2,256,2]{2,3,1,0:T(2,128)S(1)} collective-permute-done((f32[5,2,256,2]{2,3,1,0:T(2,128)S(1)}, f32[5,2,256,2]{2,3,1,0:T(2,128)S(1)}, u32[]{:S(2)}, u32[]{:S(2)}) %collective-permute-start.2) | collective-permute-done | bytes 20512 | tf_op jit(solution)/shard_map/ppermute | solution.py:14
  389.5 17.2 %collective-permute-done.1 = f32[5,2,256,96]{2,3,1,0:T(8,128)S(1)} collective-permute-done((f32[5,2,256,96]{2,3,1,0:T(8,128)}, f32[5,2,256,96]{2,3,1,0:T(8,128)S(1)}, u32[]{:S(2)}, u32[]{:S(2)}) %collective-permute-start.1) | collective-permute-done | bytes 983072 | tf_op jit(solution)/shard_map/ppermute | solution.py:26
  406.7 1.9 collective-permute-done
  409.5 2.5 fusion.49
  412.9 2.0 copy.40
  426.2 6.0 %fusion.11 = f32[5,6,260,100]{2,3,1,0:T(8,128)S(1)} fusion(f32[5,2,256,2]{2,3,1,0:T(2,128)S(1)} %broadcast_multiply_fusion.1, f32[5,6,260,2]{2,3,1,0:T(2,128)S(1)} %reshape.49, f32[5,6,2,96]{2,3,1,0:T(8,128)S(1)} %copy.42, f32[5,2,256,96]{2,3,1,0:T(8,128)S(1)} %copy-done.3, f32[5,2,256,32]{2,3,1,0:T(8,128)S(1)} %slice.186, ...), kind=kLoop, calls=%fused_computation.19 | loop fusion | flops 7020000 | bytes 6198080 | tf_op jit(solution)/shard_map/concatenate | solution.py:89
  (233 shorter events, 66.9 us)
Async XLA Ops:
  1.1 7.8 %copy-start.11 = (s32[64]{0:T(128)S(1)}, s32[64]{0:T(128)}, u32[]{:S(2)}) copy-start(s32[64]{0:T(128)} %param.10) | copy-start | bytes 772
  2.6 32.1 %all-to-all-start = ((f32[10,64,256]{2,0,1:T(8,128)}), f32[10,64,256]{2,0,1:T(8,128)S(1)}, u32[]{:S(2)}, u32[]{:S(2)}) async-start(f32[10,64,256]{2,0,1:T(8,128)} %copy.30), calls=%async_computation | async-start | bytes 2097152 | tf_op jit(solution)/shard_map/all_to_all | solution.py:147
  158.4 223.7 %all-to-all-start.1 = ((f32[4,10,16,256]{3,2,1,0:T(8,128)}), f32[4,10,16,256]{3,2,1,0:T(8,128)S(1)}, u32[]{:S(2)}, u32[]{:S(2)}) async-start(f32[4,10,16,256]{3,2,1,0:T(8,128)} %pad_maximum_fusion.4), calls=%async_computation.1 | async-start | bytes 1310720 | tf_op jit(solution)/shard_map/all_to_all | solution.py:155
  365.9 23.5 %copy-start.10 = (f32[5]{0:T(128)S(1)}, f32[5]{0:T(128)}, u32[]{:S(2)}) copy-start(f32[5]{0:T(128)} %constant.217.clone) | copy-start | bytes 64
  382.1 26.6 %copy-start = (f32[4,10,16,256]{3,2,0,1:T(8,128)}, f32[4,10,16,256]{3,2,0,1:T(8,128)S(1)}, u32[]{:S(2)}) copy-start(f32[4,10,16,256]{3,2,0,1:T(8,128)S(1)} %copy.38) | copy-start | bytes 1966084
  383.3 23.4 %collective-permute-start.1 = (f32[5,2,256,96]{2,3,1,0:T(8,128)}, f32[5,2,256,96]{2,3,1,0:T(8,128)S(1)}, u32[]{:S(2)}, u32[]{:S(2)}) collective-permute-start(f32[5,2,256,96]{2,3,1,0:T(8,128)} %pad_maximum_fusion.3), channel_id=1, source_target_pairs={{4,0},{8,4},{12,8},{16,12},{20,16},{24,20},{28,24},{0,28},{5,1},{9... | collective-permute-start | bytes 2949128 | tf_op jit(solution)/shard_map/ppermute | solution.py:26
  384.5 24.1 %collective-permute-start = (f32[5,2,256,96]{2,3,1,0:T(8,128)}, f32[5,2,256,96]{2,3,1,0:T(8,128)S(1)}, u32[]{:S(2)}, u32[]{:S(2)}) collective-permute-start(f32[5,2,256,96]{2,3,1,0:T(8,128)} %pad_maximum_fusion.3), channel_id=1, source_target_pairs={{0,4},{4,8},{8,12},{12,16},{16,20},{20,24},{24,28},{28,0},{1,5},{5... | collective-permute-start | bytes 2949128 | tf_op jit(solution)/shard_map/ppermute | solution.py:24
  384.5 4.7 %collective-permute-start.2 = (f32[5,2,256,2]{2,3,1,0:T(2,128)S(1)}, f32[5,2,256,2]{2,3,1,0:T(2,128)S(1)}, u32[]{:S(2)}, u32[]{:S(2)}) collective-permute-start(f32[5,2,256,2]{2,3,1,0:T(2,128)S(1)} %slice.238), channel_id=1, source_target_pairs={{0,2},{1,3},{2,0},{3,1},{4,6},{5,7},{6,4},{7,5},{8,10},{9,11},{10,... | collective-permute-start | bytes 61448 | tf_op jit(solution)/shard_map/ppermute | solution.py:14
  406.7 2.1 copy-start.2
  408.5 0.9 copy-start.4
  409.5 2.5 copy-start.6
  412.9 5.9 %copy-start.7 = (f32[5,6,256,96]{2,3,1,0:T(8,128)S(1)}, f32[5,6,256,96]{2,3,1,0:T(8,128)}, u32[]{:S(2)}) copy-start(f32[5,6,256,96]{2,3,1,0:T(8,128)} %copy-done.6) | copy-start | bytes 8847364
  414.8 7.8 %collective-permute-start.4 = (f32[5,6,2,96]{3,2,1,0:T(2,128)S(1)}, f32[5,6,2,96]{3,2,1,0:T(2,128)S(1)}, u32[]{:S(2)}, u32[]{:S(2)}) collective-permute-start(f32[5,6,2,96]{3,2,1,0:T(2,128)S(1)} %copy.40), channel_id=1, source_target_pairs={{1,0},{2,1},{3,2},{0,3},{5,4},{6,5},{7,6},{4,7},{9,8},{10,9},{11,1... | collective-permute-start | bytes 69128 | tf_op jit(solution)/shard_map/ppermute | solution.py:26
  418.2 5.7 %collective-permute-start.3 = (f32[5,6,2,96]{3,2,1,0:T(2,128)S(1)}, f32[5,6,2,96]{3,2,1,0:T(2,128)S(1)}, u32[]{:S(2)}, u32[]{:S(2)}) collective-permute-start(f32[5,6,2,96]{3,2,1,0:T(2,128)S(1)} %copy.39), channel_id=1, source_target_pairs={{0,1},{1,2},{2,3},{3,0},{4,5},{5,6},{6,7},{7,4},{8,9},{9,10},{10,1... | collective-permute-start | bytes 69128 | tf_op jit(solution)/shard_map/ppermute | solution.py:24
  424.4 1.4 copy-start.1
  424.4 1.5 copy-start.3
  424.4 1.8 copy-start.5
  434.0 1.8 copy-start.8
  436.8 1.2 copy-start.9
